TPU v7x, 512 devices: a whole 4x8x8 slice. The times are simulated.
512 devices in a mesh: dp: 32 (over y, x), seq: 16 (over z, core).
Axes of the slice: x: 4, y: 8, z: 8, core: 2. Of those that a mesh axis runs over, the one named last changes fastest.
Arguments:
- grad_out: bfloat16 [65536, 1280], P(('dp', 'seq')), may hold values from -6 to 6
- saved_input: bfloat16 [65536, 1280], P(('dp', 'seq')), may hold values from -6 to 6
- pre_glu: bfloat16 [65536, 2560], P(('dp', 'seq')), may hold values from -6 to 6
- queries: bfloat16 [65536, 1280], P('dp', 'seq'), may hold values from -8 to 8
- keys: bfloat16 [65536, 1280], P('dp', 'seq'), may hold values from -8 to 8
- values: bfloat16 [65536, 1280], P('dp', 'seq'), may hold values from -6 to 6
- frame_counts: int32 [32, 8], P('dp'), may hold values from 1 to 1024, 2048 in all within a row
- norm_gain: float32 [1280], replicated, may hold values from 0.5 to 1.5
- kernel: float32 [31, 1280], replicated, may hold values from -1 to 1
- w_in: bfloat16 [1280, 2560], P('dp'), may hold values from -0.15625 to 0.15625
- w_conv_out: bfloat16 [1280, 1280], P('dp'), may hold values from -0.15625 to 0.15625
- w_attn_out: bfloat16 [1280, 1280], P('dp'), may hold values from -0.15625 to 0.15625
Outputs:
- resid_grad: bfloat16 [65536, 1280], P(('dp', 'seq'))
- query_grad: bfloat16 [65536, 1280], P('dp', 'seq')
- key_grad: bfloat16 [65536, 1280], P('dp', 'seq')
- value_grad: bfloat16 [65536, 1280], P('dp', 'seq')
- kernel_grad: float32 [31, 1280], replicated
- gain_grad: float32 [1280], replicated
Inputs may be any that keep to these rules, and one draw needn't show every extreme that they name: `frame_counts`: each row sums to 2048; its largest entry is exactly 1024.
All inputs are finite; a program needn't handle non-finite values.
Results may differ from a plain program's by a relative error of at most 0.018.
Values may be sent and summed in bfloat16 or wider, within the bound.
No kernel may reach another device: no remote copies, remote signals or barrier semaphores. Data moves between devices by JAX's collectives and lax.ppermute only.
A program may use at most 64 MiB of HBM per device.

v0:
```python
import math
import jax
import jax.numpy as jnp
from jax import lax
from jax.sharding import PartitionSpec as P

HD = 80
KW = 31


def padded(block, sides, width):
    for axis, dim in sides:
        count = lax.axis_size(axis)
        forward = [(i, i + 1) for i in range(count - 1)]
        backward = [(target, source) for source, target in forward]
        low = lax.ppermute(
            lax.slice_in_dim(block, block.shape[dim] - width, None, axis=dim), axis, forward
        )
        high = lax.ppermute(lax.slice_in_dim(block, 0, width, axis=dim), axis, backward)
        block = jnp.concatenate([low, block, high], axis=dim)
    return block


def segments_of(frame_lens, positions):
    ends = jnp.cumsum(frame_lens)
    counted = jnp.sum((positions[:, None] >= ends[None, :]).astype(jnp.int32), axis=1)
    return jnp.where(positions < 0, jnp.int32(-1), counted)


def row_product(active, piece):
    return jnp.einsum("tc,rc->tr", active, piece, preferred_element_type=jnp.float32)


def attention_backward(query_rows, key_rows, value_rows, out_grad, seg_all):
    total, columns = query_rows.shape
    heads = columns // HD
    scale = 1.0 / math.sqrt(HD)
    query_heads = query_rows.reshape(total, heads, HD)
    key_heads = key_rows.reshape(total, heads, HD)
    value_heads = value_rows.reshape(total, heads, HD)
    grad_heads = out_grad.reshape(total, heads, HD)
    qblock = min(512, total)
    nblocks = total // qblock

    def block_step(block, carry):
        query_out, key_acc, value_acc = carry
        qstart = block * qblock
        query_block = lax.dynamic_slice_in_dim(query_heads, qstart, qblock, 0)
        grad_block = lax.dynamic_slice_in_dim(grad_heads, qstart, qblock, 0)
        seg_query = lax.dynamic_slice_in_dim(seg_all, qstart, qblock, 0)
        scores = (
            jnp.einsum("qhd,khd->hqk", query_block, key_heads, preferred_element_type=jnp.float32)
            * scale
        )
        scores = jnp.where((seg_query[:, None] == seg_all[None, :])[None], scores, -1e30)
        peak = jnp.max(scores, axis=2, keepdims=True)
        expd = jnp.exp(scores - peak)
        probs = expd / jnp.sum(expd, axis=2, keepdims=True)
        probs_low = probs.astype(jnp.bfloat16)
        value_part = jnp.einsum(
            "hqk,qhd->khd", probs_low, grad_block, preferred_element_type=jnp.float32
        )
        prob_grad = jnp.einsum(
            "qhd,khd->hqk", grad_block, value_heads, preferred_element_type=jnp.float32
        )
        delta = jnp.sum(probs * prob_grad, axis=2, keepdims=True)
        score_grad = (probs * (prob_grad - delta)).astype(jnp.bfloat16)
        query_part = (
            jnp.einsum("hqk,khd->qhd", score_grad, key_heads, preferred_element_type=jnp.float32)
            * scale
        ).astype(jnp.bfloat16)
        key_part = jnp.einsum(
            "hqk,qhd->khd", score_grad, query_block, preferred_element_type=jnp.float32
        )
        query_out = lax.dynamic_update_slice_in_dim(query_out, query_part, qstart, 0)
        return (query_out, key_acc + key_part, value_acc + value_part)

    initial = (
        jnp.zeros((total, heads, HD), jnp.bfloat16),
        jnp.zeros((total, heads, HD), jnp.float32),
        jnp.zeros((total, heads, HD), jnp.float32),
    )
    query_out, key_acc, value_acc = lax.fori_loop(0, nblocks, block_step, initial)
    key_grad = (key_acc * scale).astype(jnp.bfloat16)
    value_grad = value_acc.astype(jnp.bfloat16)
    return (
        query_out.reshape(total, columns),
        key_grad.reshape(total, columns),
        value_grad.reshape(total, columns),
    )


def local(
    grad_out,
    saved_input,
    pre_glu,
    queries,
    keys,
    values,
    frame_counts,
    norm_gain,
    kernel,
    w_in,
    w_conv_out,
    w_attn_out,
):
    t_dev, width = grad_out.shape
    n_seq = lax.axis_size("seq")
    total = t_dev * n_seq
    half = KW // 2
    frame_lens = frame_counts[0]
    seq_index = lax.axis_index("seq")
    ext_pos = seq_index * t_dev + jnp.arange(-half, t_dev + half, dtype=jnp.int32)
    seg_ext = segments_of(frame_lens, ext_pos)
    seg_own = seg_ext[half : half + t_dev]
    first_half = pre_glu[:, :width].astype(jnp.float32)
    gate_sig = jax.nn.sigmoid(pre_glu[:, width:].astype(jnp.float32))
    glu_out = (first_half * gate_sig).astype(jnp.bfloat16)
    glu_ext = padded(glu_out, (("seq", 0),), half).astype(jnp.float32)
    matches = [
        (seg_ext[tap_index : tap_index + t_dev] == seg_own).astype(jnp.float32)[:, None]
        for tap_index in range(KW)
    ]
    conv_out = jnp.zeros((t_dev, width), jnp.float32)
    for tap_index in range(KW):
        conv_out = (
            conv_out
            + kernel[tap_index] * glu_ext[tap_index : tap_index + t_dev] * matches[tap_index]
        )
    conv_out_grad = row_product(grad_out, lax.all_gather(w_conv_out, "dp", axis=0, tiled=True))
    conv_sig = jax.nn.sigmoid(conv_out)
    conv_grad = (conv_out_grad * conv_sig * (1.0 + conv_out * (1.0 - conv_sig))).astype(
        jnp.bfloat16
    )
    grad_ext = padded(conv_grad, (("seq", 0),), half).astype(jnp.float32)
    grad_float = grad_ext[half : half + t_dev]
    glu_grad = jnp.zeros((t_dev, width), jnp.float32)
    kernel_rows = []
    for tap_index in range(KW):
        back = 2 * half - tap_index
        glu_grad = glu_grad + kernel[tap_index] * grad_ext[back : back + t_dev] * matches[back]
        kernel_rows.append(
            jnp.sum(
                grad_float * glu_ext[tap_index : tap_index + t_dev] * matches[tap_index], axis=0
            )
        )
    glu_in_grad = jnp.concatenate(
        [glu_grad * gate_sig, glu_grad * first_half * gate_sig * (1.0 - gate_sig)], axis=1
    ).astype(jnp.bfloat16)
    norm_grad = row_product(glu_in_grad, lax.all_gather(w_in, "dp", axis=0, tiled=True))
    inputs = saved_input.astype(jnp.float32)
    centred = inputs - jnp.mean(inputs, axis=1, keepdims=True)
    inv_std = 1.0 / jnp.sqrt(jnp.mean(centred * centred, axis=1, keepdims=True) + 1e-05)
    normed = centred * inv_std
    scaled_grad = norm_grad * norm_gain
    input_grad = inv_std * (
        scaled_grad
        - jnp.mean(scaled_grad, axis=1, keepdims=True)
        - normed * jnp.mean(scaled_grad * normed, axis=1, keepdims=True)
    )
    resid_grad = (grad_out.astype(jnp.float32) + input_grad).astype(jnp.bfloat16)
    gain_term = jnp.sum(norm_grad * normed, axis=0)
    ctx_float = row_product(resid_grad, lax.all_gather(w_attn_out, "dp", axis=0, tiled=True))
    ctx_grad = ctx_float.astype(jnp.bfloat16)
    relayed = lax.all_to_all(ctx_grad, "seq", split_axis=1, concat_axis=0, tiled=True)
    seg_all = segments_of(frame_lens, jnp.arange(total, dtype=jnp.int32))
    query_grad, key_grad, value_grad = attention_backward(queries, keys, values, relayed, seg_all)
    kernel_grad, gain_grad = lax.psum((jnp.stack(kernel_rows), gain_term), ("dp", "seq"))
    return (resid_grad, query_grad, key_grad, value_grad, kernel_grad, gain_grad)


def solution(mesh):
    in_specs = (
        P(("dp", "seq"), None),
        P(("dp", "seq"), None),
        P(("dp", "seq"), None),
        P("dp", "seq"),
        P("dp", "seq"),
        P("dp", "seq"),
        P("dp", None),
        P(),
        P(),
        P("dp", None),
        P("dp", None),
        P("dp", None),
    )
    out_specs = (P(("dp", "seq"), None), P("dp", "seq"), P("dp", "seq"), P("dp", "seq"), P(), P())
    return jax.shard_map(local, mesh=mesh, in_specs=in_specs, out_specs=out_specs, check_vma=False)
```

profile of v0, /device:TPU:1, one launch (start us, length us, event | category | flops | bytes accessed | tf_op | source)
XLA Modules:
  0.0 569.4 jit_solution(128491667545102661)
XLA Ops:
  10.0 5.4 collective-permute-start
  15.4 4.7 collective-permute-start.1
  26.8 71.7 %all-gather.4.cloned.1.call-done = bf16[1280,1280]{1,0:T(8,128)(2,1)} async-done(((bf16[40,1280]{1,0:T(8,128)(2,1)}), bf16[1280,1280]{1,0:T(8,128)(2,1)}) %all-gather.4.cloned.1.call-update) | async-done | bytes 3276816 | tf_op jit(solution)/shard_map/all_gather | solution.py:130
  98.6 5.7 fusion.26
  104.3 7.3 %collective-permute-start.2 = (bf16[15,1280]{1,0:T(8,128)(2,1)S(1)}, bf16[15,1280]{1,0:T(8,128)(2,1)S(1)}, u32[]{:S(2)}, u32[]{:S(2)}) collective-permute-start(bf16[15,1280]{1,0:T(8,128)(2,1)S(1)} %get-tuple-element.284), channel_id=1, source_target_pairs={{0,1},{1,2},{2,3},{3,4},{4,5},{5,6},{6,7},{7,8},{8,9},{9,10},{10,1... | collective-permute-start | bytes 115208 | tf_op jit(solution)/shard_map/ppermute | solution.py:16
  111.6 2.1 collective-permute-start.3
  113.8 3.1 collective-permute-done.3
  119.9 4.4 multiply_convert_fusion.2
  124.5 72.3 %all-gather.6.cloned.1.call-done = bf16[1280,2560]{1,0:T(8,128)(2,1)} async-done(((bf16[40,2560]{1,0:T(8,128)(2,1)}), bf16[1280,2560]{1,0:T(8,128)(2,1)}) %all-gather.6.cloned.1.call-update) | async-done | bytes 6553616 | tf_op jit(solution)/shard_map/all_gather | solution.py:150
  196.9 5.3 fusion.37
  202.6 77.3 %all-gather.8.cloned.1.call-done = bf16[1280,1280]{1,0:T(8,128)(2,1)} async-done(((bf16[40,1280]{1,0:T(8,128)(2,1)}), bf16[1280,1280]{1,0:T(8,128)(2,1)}) %all-gather.8.cloned.1.call-update) | async-done | bytes 3276816 | tf_op jit(solution)/shard_map/all_gather | solution.py:163
  279.9 3.1 convolution_convert_fusion
  284.0 11.6 %all-to-all-start = ((bf16[128,16,80]{0,2,1:T(8,128)(2,1)}), bf16[128,16,80]{0,2,1:T(8,128)(2,1)S(1)}, u32[]{:S(2)}, u32[]{:S(2)}) async-start(bf16[128,16,80]{0,2,1:T(8,128)(2,1)} %bitcast.4), calls=%async_computation | async-start | bytes 655360 | tf_op jit(solution)/shard_map/all_to_all | solution.py:165
  297.4 2.7 stack.127
  300.1 97.6 %psum.15 = f32[1280]{0:T(1024)} all-reduce(f32[1280]{0:T(1024)S(1)} %get-tuple-element.225), channel_id=1, replica_groups=mesh['dp'=32,'seq'=16] {'dp','seq'}, use_global_device_ids=true, to_apply=%region_45.46 | all-reduce | flops 1280 | bytes 10240 | tf_op jit(solution)/shard_map/psum | solution.py:168
  398.0 44.9 %while.18 = (s32[]{:T(128)}, bf16[2048,1,80]{0,2,1:T(8,128)(2,1)S(1)}, f32[2048,1,80]{0,2,1:T(8,128)S(1)}, f32[2048,1,80]{0,2,1:T(8,128)}, s32[2048]{0:T(1024)S(...) while((s32[]{:T(128)}, ...), condition=%wide.region_11.12_spmd.clone, body=%wide.region_7.0_spmd.clone.sunk | while | flops 858470912 | bytes 79810904 | solution.py:83
  399.1 1.9 copy-done
  401.8 3.4 fusion.141
  410.3 1.9 copy-done
  413.0 3.4 fusion.141
  424.2 3.4 fusion.141
  435.4 3.4 fusion.141
  442.9 2.0 convert_bitcast_fusion
  445.6 115.7 %all-reduce.2.cloned.1.call-done = f32[31,1280]{1,0:T(8,128)} async-done(((f32[31,1280]{1,0:T(8,128)}), f32[31,1280]{1,0:T(8,128)}) %all-reduce.2.cloned.1.call-update) | async-done | bytes 158736 | tf_op jit(solution)/shard_map/psum | solution.py:168
  (161 shorter events, 45.5 us)
Async XLA Ops:
  7.2 91.4 %all-gather.4.cloned.1.call-start = ((), (), s32[]{:S(2)}) async-start(), calls=%async_computation.1 | async-start | bytes 3379200 | tf_op jit(solution)/shard_map/all_gather | solution.py:130
  7.9 189.0 %all-gather.6.cloned.1.call-start = ((), (), s32[]{:S(2)}) async-start(), calls=%async_computation.2 | async-start | bytes 6758400 | tf_op jit(solution)/shard_map/all_gather | solution.py:150
  8.6 271.3 %all-gather.8.cloned.1.call-start = ((), (), s32[]{:S(2)}) async-start(), calls=%async_computation.3 | async-start | bytes 3379200 | tf_op jit(solution)/shard_map/all_gather | solution.py:163
  10.0 16.7 %collective-permute-start = (bf16[15,1280]{1,0:T(8,128)(2,1)S(1)}, bf16[15,1280]{1,0:T(8,128)(2,1)S(1)}, u32[]{:S(2)}, u32[]{:S(2)}) collective-permute-start(bf16[15,1280]{1,0:T(8,128)(2,1)S(1)} %get-tuple-element.286), channel_id=1, source_target_pairs={{0,1},{1,2},{2,3},{3,4},{4,5},{5,6},{6,7},{7,8},{8,9},{9,10},{10,1... | collective-permute-start | bytes 115208 | tf_op jit(solution)/shard_map/ppermute | solution.py:16
  15.4 11.3 %collective-permute-start.1 = (bf16[15,1280]{1,0:T(8,128)(2,1)S(1)}, bf16[15,1280]{1,0:T(8,128)(2,1)S(1)}, u32[]{:S(2)}, u32[]{:S(2)}) collective-permute-start(bf16[15,1280]{1,0:T(8,128)(2,1)S(1)} %get-tuple-element.287), channel_id=1, source_target_pairs={{1,0},{2,1},{3,2},{4,3},{5,4},{6,5},{7,6},{8,7},{9,8},{10,9},{11,1... | collective-permute-start | bytes 115208 | tf_op jit(solution)/shard_map/ppermute | solution.py:19
  104.3 9.6 %collective-permute-start.2 = (bf16[15,1280]{1,0:T(8,128)(2,1)S(1)}, bf16[15,1280]{1,0:T(8,128)(2,1)S(1)}, u32[]{:S(2)}, u32[]{:S(2)}) collective-permute-start(bf16[15,1280]{1,0:T(8,128)(2,1)S(1)} %get-tuple-element.284), channel_id=1, source_target_pairs={{0,1},{1,2},{2,3},{3,4},{4,5},{5,6},{6,7},{7,8},{8,9},{9,10},{10,1... | collective-permute-start | bytes 115208 | tf_op jit(solution)/shard_map/ppermute | solution.py:16
  111.6 5.3 collective-permute-start.3
  119.9 77.0 %copy-start.4 = (bf16[128,1280]{1,0:T(8,128)(2,1)S(1)}, bf16[128,1280]{1,0:T(8,128)(2,1)}, u32[]{:S(2)}) copy-start(bf16[128,1280]{1,0:T(8,128)(2,1)} %param.15) | copy-start | bytes 983044
  119.9 77.0 %copy-start.11 = (f32[1280]{0:T(1024)S(1)}, f32[1280]{0:T(1024)}, u32[]{:S(2)}) copy-start(f32[1280]{0:T(1024)} %param.21) | copy-start | bytes 15364
  196.9 5.4 copy-start.10
  202.6 93.8 %copy-start.5 = (bf16[128,1280]{1,0:T(8,128)(2,1)}, bf16[128,1280]{1,0:T(8,128)(2,1)S(1)}, u32[]{:S(2)}) copy-start(bf16[128,1280]{1,0:T(8,128)(2,1)S(1)} %fusion.36) | copy-start | bytes 983044
  284.0 113.7 %all-to-all-start = ((bf16[128,16,80]{0,2,1:T(8,128)(2,1)}), bf16[128,16,80]{0,2,1:T(8,128)(2,1)S(1)}, u32[]{:S(2)}, u32[]{:S(2)}) async-start(bf16[128,16,80]{0,2,1:T(8,128)(2,1)} %bitcast.4), calls=%async_computation | async-start | bytes 655360 | tf_op jit(solution)/shard_map/all_to_all | solution.py:165
  295.5 265.8 %all-reduce.2.cloned.1.call-start = ((), (), s32[]{:S(2)}) async-start(), calls=%async_computation.4 | async-start | bytes 327680 | tf_op jit(solution)/shard_map/psum | solution.py:168
  296.4 101.5 %copy-start.2 = (bf16[2048,80]{0,1:T(8,128)(2,1)S(1)}, bf16[2048,80]{0,1:T(8,128)(2,1)}, u32[]{:S(2)}) copy-start(bf16[2048,80]{0,1:T(8,128)(2,1)} %param.18) | copy-start | bytes 983044
  296.4 101.5 %copy-start.8 = (bf16[2048,80]{0,1:T(8,128)(2,1)S(1)}, bf16[2048,80]{0,1:T(8,128)(2,1)}, u32[]{:S(2)}) copy-start(bf16[2048,80]{0,1:T(8,128)(2,1)} %param.17) | copy-start | bytes 983044
  398.1 3.7 copy-start.6
  401.8 3.5 copy-start.12
  409.3 3.7 copy-start.6
  413.0 3.5 copy-start.12
  420.5 3.7 copy-start.6
  424.2 3.5 copy-start.12
  431.8 3.7 copy-start.6
  435.4 3.5 copy-start.12
  442.9 120.0 %copy-start.9 = (bf16[2048,1,80]{0,2,1:T(8,128)(2,1)}, bf16[2048,1,80]{0,2,1:T(8,128)(2,1)S(1)}, u32[]{:S(2)}) copy-start(bf16[2048,1,80]{0,2,1:T(8,128)(2,1)S(1)} %get-tuple-element.162) | copy-start | bytes 983044
  (13 other events, 28.8 us)
Sparse Core Ops, SparseCore 0:
  11.2 87.3 all-gather.3
  101.7 95.0 all-gather.5
  200.0 79.8 all-gather.7
  301.6 259.6 all-reduce.1
where the time goes:
time: 570 us; the launch traced here: 569 us
  waiting for transfers between devices  342 us (60%)
  blocking collectives  97.6 us (17%)
  matrix products  42 us (7%)
  starting transfers between devices  31.2 us (5%)
  other arithmetic  25.2 us (4%)
  local copies, waits for them, and re-layouts  17.2 us (3%)
  between operations  14.3 us (3%)
    psum x1, waiting for transfers between devices, local(): lax.psum((jnp.stack(kernel_rows), gain_term), ('dp', 'seq'))  116 us
    psum x1, blocking collectives, local(): lax.psum((jnp.stack(kernel_rows), gain_term), ('dp', 'seq'))  97.6 us
    all_gather x1, waiting for transfers between devices, local(): lax.all_gather(w_attn_out, 'dp', axis=0, tiled=True)  77.3 us
    all_gather x1, waiting for transfers between devices, local(): lax.all_gather(w_in, 'dp', axis=0, tiled=True)  72.3 us
    all_gather x1, waiting for transfers between devices, local(): lax.all_gather(w_conv_out, 'dp', axis=0, tiled=True)  71.7 us
    dot_general x3, matrix products, row_product(): jnp.einsum('tc,rc->tr', active, piece, preferred_element_type=jnp.float32)  14.2 us
    dot_general x4, matrix products, block_step(): jnp.einsum('hqk,qhd->khd', probs_low, grad_block, preferred_element_type=...  13.4 us
    ppermute x2, starting transfers between devices, padded(): lax.ppermute(lax.slice_in_dim(block, block.shape[dim] - width, None, axis...  12.7 us
  transfers between devices with their start and end apart: 9, of which 5 were waited for; matrix products, arithmetic and copies ran while one was open for 12% of the time, Pallas kernels for 0%

commit v1 on v0

--- a/solution.py
+++ b/solution.py
@@ -6,6 +6,11 @@
 
 HD = 80
 KW = 31
+
+
+def gather_from_all(shard, axis, dim):
+    copies = jnp.concatenate([shard] * lax.axis_size(axis), axis=dim)
+    return lax.all_to_all(copies, axis, dim, dim, tiled=True)
 
 
 def padded(block, sides, width):
@@ -147,7 +152,7 @@
     glu_in_grad = jnp.concatenate(
         [glu_grad * gate_sig, glu_grad * first_half * gate_sig * (1.0 - gate_sig)], axis=1
     ).astype(jnp.bfloat16)
-    norm_grad = row_product(glu_in_grad, lax.all_gather(w_in, "dp", axis=0, tiled=True))
+    norm_grad = row_product(glu_in_grad, gather_from_all(w_in, "dp", 0))
     inputs = saved_input.astype(jnp.float32)
     centred = inputs - jnp.mean(inputs, axis=1, keepdims=True)
     inv_std = 1.0 / jnp.sqrt(jnp.mean(centred * centred, axis=1, keepdims=True) + 1e-05)

time: 570 us -> 549 us (0.963)
  waiting for transfers between devices: 342 us -> 288 us
  local copies, waits for them, and re-layouts: 17.2 us -> 44.4 us
    all_gather x1 -> x0, waiting for transfers between devices: 72.3 us -> none  [local(): lax.all_gather(w_in, 'dp', axis=0, tiled=True)]
    all_gather x1, waiting for transfers between devices: 77.3 us -> 48.7 us  [local(): lax.all_gather(w_attn_out, 'dp', axis=0, tiled=True)]
    all_gather x1, waiting for transfers between devices: 71.7 us -> 99.9 us  [local(): lax.all_gather(w_conv_out, 'dp', axis=0, tiled=True)]
    unnamed x17 -> x276, local copies, waits for them, and re-layouts: 1.64 us -> 20.2 us
    all_to_all x0 -> x1, waiting for transfers between devices: none -> 18.4 us  [gather_from_all(): return lax.all_to_all(copies, axis, dim, dim, tiled=True)]
    another operation x32, local copies, waits for them, and re-layouts: 2.87 us -> 14.1 us  [local(): jnp.stack(kernel_rows)]
    all_to_all x0 -> x1, starting transfers between devices: none -> 10.8 us  [gather_from_all(): return lax.all_to_all(copies, axis, dim, dim, tiled=True)]
  transfers between devices with their start and end apart: 9 -> 9, of which waited for: 5 -> 6; matrix products, arithmetic and copies ran while one was open for 12% -> 17% of each run, Pallas kernels for 0% -> 0%
where the time goes in v1:
time: 549 us; the launch traced here: 548 us
  waiting for transfers between devices  288 us (52%)
  blocking collectives  97.9 us (18%)
  local copies, waits for them, and re-layouts  44.4 us (8%)
  matrix products  41.9 us (8%)
  starting transfers between devices  34.2 us (6%)
  other arithmetic  25.3 us (5%)
  between operations  16 us (3%)
    psum x1, waiting for transfers between devices, local(): lax.psum((jnp.stack(kernel_rows), gain_term), ('dp', 'seq'))  116 us
    all_gather x1, waiting for transfers between devices, local(): lax.all_gather(w_conv_out, 'dp', axis=0, tiled=True)  99.9 us
    psum x1, blocking collectives, local(): lax.psum((jnp.stack(kernel_rows), gain_term), ('dp', 'seq'))  97.9 us
    all_gather x1, waiting for transfers between devices, local(): lax.all_gather(w_attn_out, 'dp', axis=0, tiled=True)  48.7 us
    unnamed x276, local copies, waits for them, and re-layouts  20.2 us
    all_to_all x1, waiting for transfers between devices, gather_from_all(): return lax.all_to_all(copies, axis, dim, dim, tiled=True)  18.4 us
    dot_general x3, matrix products, row_product(): jnp.einsum('tc,rc->tr', active, piece, preferred_element_type=jnp.float32)  14.1 us
    another operation x32, local copies, waits for them, and re-layouts, local(): jnp.stack(kernel_rows)  14.1 us
  transfers between devices with their start and end apart: 9, of which 6 were waited for; matrix products, arithmetic and copies ran while one was open for 17% of the time, Pallas kernels for 0%

profile of v1, /device:TPU:1, one launch (start us, length us, event | category | flops | bytes accessed | tf_op | source)
XLA Modules:
  0.0 548.2 jit_solution(6226409925934442227)
XLA Ops:
  23.5 2.7 copy-done.4
  26.2 10.8 %all-to-all-start = ((bf16[32,40,2560]{2,1,0:T(8,128)(2,1)}), bf16[32,40,2560]{2,1,0:T(8,128)(2,1)}, u32[]{:S(2)}, u32[]{:S(2)}) async-start(bf16[32,40,2560]{2,1,0:T(8,128)(2,1)} %bitcast.94), calls=%async_computation | async-start | bytes 13107200 | tf_op jit(solution)/shard_map/all_to_all | solution.py:13
  37.2 4.8 collective-permute-start
  47.9 99.9 %all-gather.3.cloned.1.call-done = bf16[1280,1280]{1,0:T(8,128)(2,1)} async-done(((bf16[40,1280]{1,0:T(8,128)(2,1)}), bf16[1280,1280]{1,0:T(8,128)(2,1)}) %all-gather.3.cloned.1.call-update) | async-done | bytes 3276816 | tf_op jit(solution)/shard_map/all_gather | solution.py:135
  147.8 5.6 %fusion.26 = bf16[128,1280]{1,0:T(8,128)(2,1)S(1)} fusion(bf16[128,1280]{1,0:T(8,128)(2,1)S(1)} %copy-done.13, bf16[1280,1280]{1,0:T(8,128)(2,1)} %all-gather.3.cloned.1.call-done, f32[158,1280]{1,0:T(8,128)S(1)} %maximum_convert_fusion, f32[128]{0:T(128)S(1)} %get-tuple-element.316, f32[1280]{0:T(1024)S(1)} %get-tuple-element.257, ...), kind=kOutput, calls=%fused_computation.33 | convolution fusion | flops 435814400 | bytes 24422400 | tf_op jit(solution)/shard_map/tc,rc->tr/dot_general | solution.py:36
  153.8 2.9 collective-permute-start.2
  156.7 2.1 collective-permute-start.3
  159.1 3.4 collective-permute-done.3
  178.6 4.4 multiply_convert_fusion.2
  184.0 18.4 %all-to-all-done = bf16[32,40,2560]{2,1,0:T(8,128)(2,1)} async-done(((bf16[32,40,2560]{2,1,0:T(8,128)(2,1)}), bf16[32,40,2560]{2,1,0:T(8,128)(2,1)}, u32[]{:S(2)}, u32[]{:S(2)}) %all-to-all-start) | async-done | bytes 6553632 | tf_op jit(solution)/shard_map/all_to_all | solution.py:13
  202.5 5.4 fusion.37
  209.4 48.7 %all-gather.5.cloned.1.call-done = bf16[1280,1280]{1,0:T(8,128)(2,1)} async-done(((bf16[40,1280]{1,0:T(8,128)(2,1)}), bf16[1280,1280]{1,0:T(8,128)(2,1)}) %all-gather.5.cloned.1.call-update) | async-done | bytes 3276816 | tf_op jit(solution)/shard_map/all_gather | solution.py:168
  258.1 3.1 convolution_convert_fusion
  262.1 11.6 %all-to-all-start.1 = ((bf16[128,16,80]{0,2,1:T(8,128)(2,1)}), bf16[128,16,80]{0,2,1:T(8,128)(2,1)S(1)}, u32[]{:S(2)}, u32[]{:S(2)}) async-start(bf16[128,16,80]{0,2,1:T(8,128)(2,1)} %bitcast.6), calls=%async_computation.1 | async-start | bytes 655360 | tf_op jit(solution)/shard_map/all_to_all | solution.py:170
  275.8 2.7 stack.127
  278.5 97.9 %psum.15 = f32[1280]{0:T(1024)} all-reduce(f32[1280]{0:T(1024)S(1)} %get-tuple-element.225), channel_id=1, replica_groups=mesh['dp'=32,'seq'=16] {'dp','seq'}, use_global_device_ids=true, to_apply=%region_45.46 | all-reduce | flops 1280 | bytes 10240 | tf_op jit(solution)/shard_map/psum | solution.py:173
  376.7 44.9 %while.18 = (s32[]{:T(128)}, bf16[2048,1,80]{0,2,1:T(8,128)(2,1)S(1)}, f32[2048,1,80]{0,2,1:T(8,128)S(1)}, f32[2048,1,80]{0,2,1:T(8,128)}, s32[2048]{0:T(1024)S(...) while((s32[]{:T(128)}, ...), condition=%wide.region_11.12_spmd.clone, body=%wide.region_7.0_spmd.clone.sunk | while | flops 858470912 | bytes 79810904 | solution.py:88
  377.8 1.9 copy-done
  380.5 3.4 fusion.141
  391.7 3.4 fusion.141
  402.9 3.4 fusion.141
  414.1 3.4 fusion.141
  421.6 2.0 convert_bitcast_fusion
  424.3 115.7 %all-reduce.2.cloned.1.call-done = f32[31,1280]{1,0:T(8,128)} async-done(((f32[31,1280]{1,0:T(8,128)}), f32[31,1280]{1,0:T(8,128)}) %all-reduce.2.cloned.1.call-update) | async-done | bytes 158736 | tf_op jit(solution)/shard_map/psum | solution.py:173
  (420 shorter events, 74.6 us)
Async XLA Ops:
  7.2 140.6 %all-gather.3.cloned.1.call-start = ((), (), s32[]{:S(2)}) async-start(), calls=%async_computation.2 | async-start | bytes 3379200 | tf_op jit(solution)/shard_map/all_gather | solution.py:135
  26.2 121.6 %copy-start.13 = (bf16[128,1280]{1,0:T(8,128)(2,1)S(1)}, bf16[128,1280]{1,0:T(8,128)(2,1)}, u32[]{:S(2)}) copy-start(bf16[128,1280]{1,0:T(8,128)(2,1)} %param.14) | copy-start | bytes 983044
  26.2 176.2 %all-to-all-start = ((bf16[32,40,2560]{2,1,0:T(8,128)(2,1)}), bf16[32,40,2560]{2,1,0:T(8,128)(2,1)}, u32[]{:S(2)}, u32[]{:S(2)}) async-start(bf16[32,40,2560]{2,1,0:T(8,128)(2,1)} %bitcast.94), calls=%async_computation | async-start | bytes 13107200 | tf_op jit(solution)/shard_map/all_to_all | solution.py:13
  37.0 221.1 %all-gather.5.cloned.1.call-start = ((), (), s32[]{:S(2)}) async-start(), calls=%async_computation.3 | async-start | bytes 3379200 | tf_op jit(solution)/shard_map/all_gather | solution.py:168
  37.2 9.1 %collective-permute-start = (bf16[15,1280]{1,0:T(8,128)(2,1)S(1)}, bf16[15,1280]{1,0:T(8,128)(2,1)S(1)}, u32[]{:S(2)}, u32[]{:S(2)}) collective-permute-start(bf16[15,1280]{1,0:T(8,128)(2,1)S(1)} %get-tuple-element.286), channel_id=1, source_target_pairs={{0,1},{1,2},{2,3},{3,4},{4,5},{5,6},{6,7},{7,8},{8,9},{9,10},{10,1... | collective-permute-start | bytes 115208 | tf_op jit(solution)/shard_map/ppermute | solution.py:21
  42.1 5.7 %collective-permute-start.1 = (bf16[15,1280]{1,0:T(8,128)(2,1)S(1)}, bf16[15,1280]{1,0:T(8,128)(2,1)S(1)}, u32[]{:S(2)}, u32[]{:S(2)}) collective-permute-start(bf16[15,1280]{1,0:T(8,128)(2,1)S(1)} %get-tuple-element.287), channel_id=1, source_target_pairs={{1,0},{2,1},{3,2},{4,3},{5,4},{6,5},{7,6},{8,7},{9,8},{10,9},{11,1... | collective-permute-start | bytes 115208 | tf_op jit(solution)/shard_map/ppermute | solution.py:24
  45.6 107.8 %copy-start.66 = (f32[128]{0:T(128)}, f32[128]{0:T(128)S(1)}, u32[]{:S(2)}) copy-start(f32[128]{0:T(128)S(1)} %get-tuple-element.315) | copy-start | bytes 1540
  45.6 107.8 %copy-start.84 = (f32[128]{0:T(128)}, f32[128]{0:T(128)S(1)}, u32[]{:S(2)}) copy-start(f32[128]{0:T(128)S(1)} %get-tuple-element.316) | copy-start | bytes 1540
  45.6 107.8 %copy-start.86 = (f32[128]{0:T(128)}, f32[128]{0:T(128)S(1)}, u32[]{:S(2)}) copy-start(f32[128]{0:T(128)S(1)} %get-tuple-element.317) | copy-start | bytes 1540
  45.7 107.8 %copy-start.69 = (f32[128]{0:T(128)}, f32[128]{0:T(128)S(1)}, u32[]{:S(2)}) copy-start(f32[128]{0:T(128)S(1)} %get-tuple-element.288) | copy-start | bytes 1540
  45.7 107.8 %copy-start.88 = (f32[128]{0:T(128)}, f32[128]{0:T(128)S(1)}, u32[]{:S(2)}) copy-start(f32[128]{0:T(128)S(1)} %get-tuple-element.289) | copy-start | bytes 1540
  45.7 107.8 %copy-start.90 = (f32[128]{0:T(128)}, f32[128]{0:T(128)S(1)}, u32[]{:S(2)}) copy-start(f32[128]{0:T(128)S(1)} %get-tuple-element.290) | copy-start | bytes 1540
  45.7 107.8 %copy-start.92 = (f32[128]{0:T(128)}, f32[128]{0:T(128)S(1)}, u32[]{:S(2)}) copy-start(f32[128]{0:T(128)S(1)} %get-tuple-element.291) | copy-start | bytes 1540
  45.7 107.8 %copy-start.94 = (f32[128]{0:T(128)}, f32[128]{0:T(128)S(1)}, u32[]{:S(2)}) copy-start(f32[128]{0:T(128)S(1)} %get-tuple-element.292) | copy-start | bytes 1540
  45.7 107.8 %copy-start.96 = (f32[128]{0:T(128)}, f32[128]{0:T(128)S(1)}, u32[]{:S(2)}) copy-start(f32[128]{0:T(128)S(1)} %get-tuple-element.293) | copy-start | bytes 1540
  45.7 107.8 %copy-start.98 = (f32[128]{0:T(128)}, f32[128]{0:T(128)S(1)}, u32[]{:S(2)}) copy-start(f32[128]{0:T(128)S(1)} %get-tuple-element.294) | copy-start | bytes 1540
  45.7 107.8 %copy-start.100 = (f32[128]{0:T(128)}, f32[128]{0:T(128)S(1)}, u32[]{:S(2)}) copy-start(f32[128]{0:T(128)S(1)} %get-tuple-element.295) | copy-start | bytes 1540
  153.8 5.3 collective-permute-start.2
  156.7 5.7 %collective-permute-start.3 = (bf16[15,1280]{1,0:T(8,128)(2,1)S(1)}, bf16[15,1280]{1,0:T(8,128)(2,1)S(1)}, u32[]{:S(2)}, u32[]{:S(2)}) collective-permute-start(bf16[15,1280]{1,0:T(8,128)(2,1)S(1)} %get-tuple-element.285), channel_id=1, source_target_pairs={{1,0},{2,1},{3,2},{4,3},{5,4},{6,5},{7,6},{8,7},{9,8},{10,9},{11,1... | collective-permute-start | bytes 115208 | tf_op jit(solution)/shard_map/ppermute | solution.py:24
  261.2 115.5 %copy-start.3 = (bf16[2048,80]{0,1:T(8,128)(2,1)S(1)}, bf16[2048,80]{0,1:T(8,128)(2,1)}, u32[]{:S(2)}) copy-start(bf16[2048,80]{0,1:T(8,128)(2,1)} %param.18) | copy-start | bytes 983044
  261.2 115.5 %copy-start.10 = (bf16[2048,80]{0,1:T(8,128)(2,1)S(1)}, bf16[2048,80]{0,1:T(8,128)(2,1)}, u32[]{:S(2)}) copy-start(bf16[2048,80]{0,1:T(8,128)(2,1)} %param.17) | copy-start | bytes 983044
  262.1 114.3 %all-to-all-start.1 = ((bf16[128,16,80]{0,2,1:T(8,128)(2,1)}), bf16[128,16,80]{0,2,1:T(8,128)(2,1)S(1)}, u32[]{:S(2)}, u32[]{:S(2)}) async-start(bf16[128,16,80]{0,2,1:T(8,128)(2,1)} %bitcast.6), calls=%async_computation.1 | async-start | bytes 655360 | tf_op jit(solution)/shard_map/all_to_all | solution.py:170
  273.7 266.4 %all-reduce.2.cloned.1.call-start = ((), (), s32[]{:S(2)}) async-start(), calls=%async_computation.4 | async-start | bytes 327680 | tf_op jit(solution)/shard_map/psum | solution.py:173
  421.6 120.1 %copy-start.12 = (bf16[2048,1,80]{0,2,1:T(8,128)(2,1)}, bf16[2048,1,80]{0,2,1:T(8,128)(2,1)S(1)}, u32[]{:S(2)}) copy-start(bf16[2048,1,80]{0,2,1:T(8,128)(2,1)S(1)} %get-tuple-element.162) | copy-start | bytes 983044
  (127 other events, 5743.6 us)
Sparse Core Ops, SparseCore 0:
  11.2 136.5 all-gather.2
  151.0 107.0 all-gather.4
  280.1 259.9 all-reduce.1
